TPU v7x, 32 devices: a whole 2x2x4 slice. The times are simulated.
32 devices in a mesh: batch: 4 (over x, core), head: 8 (over z, y).
Axes of the slice: x: 2, y: 2, z: 4, core: 2. Of those that a mesh axis runs over, the one named last changes fastest.
Arguments:
- tokens: bfloat16 [5120, 2048], P('batch'), may hold values from -6 to 6
- segment_ids: int32 [5120], P('batch'), may hold values from 0 to 6, as said below
- norm1_gain: bfloat16 [2048], P('batch'), may hold values from 0.25 to 1.75
- w_query: bfloat16 [2048, 1024], P('batch', 'head'), may hold values from -0.125 to 0.125
- w_key: bfloat16 [2048, 512], P('batch', 'head'), may hold values from -0.125 to 0.125
- w_value: bfloat16 [2048, 512], P('batch', 'head'), may hold values from -0.125 to 0.125
- w_gate: bfloat16 [2048, 1024], P('batch', 'head'), may hold values from -0.125 to 0.125
- w_out: bfloat16 [1024, 2048], P('head', 'batch'), may hold values from -4 to 4
- norm2_gain: bfloat16 [2048], P('batch'), may hold values from 0.25 to 1.75
- w_mlp_gate: bfloat16 [2048, 6144], P('batch', 'head'), may hold values from -0.125 to 0.125
- w_mlp_up: bfloat16 [2048, 6144], P('batch', 'head'), may hold values from -0.125 to 0.125
- w_down: bfloat16 [6144, 2048], P('head', 'batch'), may hold values from -0.078125 to 0.078125
- out_grad: bfloat16 [5120, 2048], P('batch'), may hold values from -6 to 6
Outputs:
- output: bfloat16 [5120, 2048], P('batch')
- d_tokens: bfloat16 [5120, 2048], P('batch')
- d_norm1_gain: float32 [2048], P('batch')
- d_w_query: float32 [2048, 1024], P('batch', 'head')
- d_w_key: float32 [2048, 512], P('batch', 'head')
- d_w_value: float32 [2048, 512], P('batch', 'head')
- d_w_gate: float32 [2048, 1024], P('batch', 'head')
- d_w_out: float32 [1024, 2048], P('head', 'batch')
- d_norm2_gain: float32 [2048], P('batch')
- d_w_mlp_gate: float32 [2048, 6144], P('batch', 'head')
- d_w_mlp_up: float32 [2048, 6144], P('batch', 'head')
- d_w_down: float32 [6144, 2048], P('head', 'batch')
Inputs may be any that keep to these rules, and one draw needn't show every extreme that they name: `segment_ids`: segment ids never fall along the packed batch and every id from 0 to 6 occurs.
All inputs are finite; a program needn't handle non-finite values.
Results may differ from a plain program's by a relative error of at most 0.02.
Values may be sent and summed in bfloat16 or wider, within the bound.
A program may use at most 256 MiB of HBM per device.

v0:
```python
import math
import jax
import jax.numpy as jnp
from jax import lax
from jax.sharding import PartitionSpec as P

EPSILON = 1e-06
MASKED = -1e30
BF = jnp.bfloat16
F32 = jnp.float32


def from_partner(block, axis):
    count = lax.axis_size(axis)
    route = [(at, at ^ 1) for at in range(count)]
    return lax.ppermute(block, axis, route)


def matmul(left, right):
    return jnp.dot(left, right, preferred_element_type=F32)


def rows_inner(left, right):
    return lax.dot_general(left, right, (((0,), (0,)), ((), ())), preferred_element_type=F32)


def cols_inner(left, right):
    return lax.dot_general(left, right, (((1,), (1,)), ((), ())), preferred_element_type=F32)


def rms_scale(values):
    return lax.rsqrt(jnp.mean(values * values, axis=1, keepdims=True) + EPSILON)


def keep_same(state):
    return state


def order_halves(own, mate, first):
    return jnp.where(first, jnp.concatenate([own, mate], 1), jnp.concatenate([mate, own], 1))


def per_device(
    tokens,
    segment_ids,
    norm1_gain,
    w_query,
    w_key,
    w_value,
    w_gate,
    w_out,
    norm2_gain,
    w_mlp_gate,
    w_mlp_up,
    w_down,
    out_grad,
):
    heads = lax.axis_size("head")
    batches = lax.axis_size("batch")
    row_count, width = tokens.shape
    head_size = w_query.shape[1]
    half = w_key.shape[1]
    chunk = row_count // heads
    me = lax.axis_index("head")
    first = me % 2 == 0
    scale_factor = 1.0 / math.sqrt(head_size)
    kv_shard = jnp.concatenate([w_key, w_value], axis=1)
    kv_mate = from_partner(kv_shard, "head")
    w_in = jnp.concatenate(
        [
            w_query,
            order_halves(w_key, kv_mate[:, :half], first),
            order_halves(w_value, kv_mate[:, half:], first),
            w_gate,
        ],
        axis=1,
    )
    w_in = lax.all_gather(w_in, "batch", axis=0, tiled=True)
    gains = lax.all_gather(jnp.stack([norm1_gain, norm2_gain]), "batch", axis=1, tiled=True)
    gain_one = gains[0].astype(F32)
    gain_two = gains[1].astype(F32)
    out_own = lax.all_gather(w_out, "batch", axis=1, tiled=True)
    out_full = lax.all_gather(out_own, "head", axis=0, tiled=True)
    mgate_full = lax.all_gather(w_mlp_gate, "batch", axis=0, tiled=True)
    mup_full = lax.all_gather(w_mlp_up, "batch", axis=0, tiled=True)
    down_full = lax.all_gather(w_down, "batch", axis=1, tiled=True)
    positions = lax.axis_index("batch") * row_count + jnp.arange(row_count, dtype=jnp.int32)
    inputs = tokens.astype(F32)
    recip_one = rms_scale(inputs)
    normed_one = (inputs * recip_one * gain_one).astype(BF)
    projected = matmul(normed_one, w_in)
    queries = projected[:, :head_size].astype(BF)
    kv_local = projected[:, head_size : 3 * head_size].astype(BF)
    gate_vals = jax.nn.sigmoid(projected[:, 3 * head_size :])
    kv_all = lax.all_gather(kv_local, "batch", axis=0, tiled=True)
    seg_all = lax.all_gather(segment_ids, "batch", axis=0, tiled=True)
    block_rows = row_count
    block_total = batches

    def block_parts(block_index):
        first_row = block_index * block_rows
        key_block = kv_all[first_row : first_row + block_rows, :head_size]
        value_block = kv_all[first_row : first_row + block_rows, head_size:]
        seg_block = seg_all[first_row : first_row + block_rows]
        key_pos = first_row + jnp.arange(block_rows, dtype=jnp.int32)
        allowed = (segment_ids[:, None] == seg_block[None, :]) & (
            key_pos[None, :] <= positions[:, None]
        )
        scores = cols_inner(queries, key_block) * scale_factor
        return (scores, allowed, key_block, value_block)

    def is_live(block_index):
        first_row = block_index * block_rows
        return (first_row <= positions[-1]) & (
            seg_all[first_row + block_rows - 1] >= segment_ids[0]
        )

    run_max = jnp.full((row_count,), MASKED, F32)
    run_sum = jnp.zeros((row_count,), F32)
    for block_index in range(block_total):

        def grow(state, block_index=block_index):
            old_max, old_sum = state
            scores, allowed, key_block, value_block = block_parts(block_index)
            new_max = jnp.maximum(old_max, jnp.max(jnp.where(allowed, scores, MASKED), axis=1))
            weights = jnp.where(allowed, jnp.exp(scores - new_max[:, None]), 0.0)
            return (new_max, old_sum * jnp.exp(old_max - new_max) + jnp.sum(weights, axis=1))

        run_max, run_sum = lax.cond(is_live(block_index), grow, keep_same, (run_max, run_sum))
    log_total = run_max + jnp.log(run_sum)

    def probs_of(block_index):
        scores, allowed, key_block, value_block = block_parts(block_index)
        return (
            jnp.where(allowed, jnp.exp(scores - log_total[:, None]), 0.0),
            key_block,
            value_block,
        )

    attended = jnp.zeros((row_count, head_size), F32)
    for block_index in range(block_total):

        def accumulate(running, block_index=block_index):
            probs, key_block, value_block = probs_of(block_index)
            return running + matmul(probs.astype(BF), value_block)

        attended = lax.cond(is_live(block_index), accumulate, keep_same, attended)
    mixed = (attended * gate_vals).astype(BF)
    mixed_all = lax.all_gather(mixed, "head", axis=1, tiled=True)
    resid = inputs + matmul(mixed_all, out_full)
    recip_two = rms_scale(resid)
    normed_two = (resid * recip_two * gain_two).astype(BF)
    resid_own = lax.dynamic_slice_in_dim(resid, me * chunk, chunk, 0)
    recip_own = lax.dynamic_slice_in_dim(recip_two, me * chunk, chunk, 0)
    mixed_own = lax.dynamic_slice_in_dim(mixed_all, me * chunk, chunk, 0)
    dy_own = lax.dynamic_slice_in_dim(out_grad, me * chunk, chunk, 0).astype(F32)
    gate_pre = matmul(normed_two, mgate_full)
    up_pre = matmul(normed_two, mup_full)
    sig_gate = jax.nn.sigmoid(gate_pre)
    silu_gate = gate_pre * sig_gate
    hidden = (silu_gate * up_pre).astype(BF)
    d_hidden = cols_inner(out_grad, down_full)
    d_gate_pre = (d_hidden * up_pre * sig_gate * (1.0 + gate_pre * (1.0 - sig_gate))).astype(BF)
    d_up_pre = (d_hidden * silu_gate).astype(BF)
    dn2_part = cols_inner(d_gate_pre, mgate_full) + cols_inner(d_up_pre, mup_full)
    dn2 = lax.psum_scatter(dn2_part.astype(BF), "head", scatter_dimension=0, tiled=True).astype(F32)
    mlp_part = matmul(hidden, down_full).astype(BF)
    mlp_own = lax.psum_scatter(mlp_part, "head", scatter_dimension=0, tiled=True).astype(F32)
    output = lax.all_gather((resid_own + mlp_own).astype(BF), "head", axis=0, tiled=True)
    d_gain_two = jnp.sum(dn2 * resid_own * recip_own, axis=0)
    weighted_two = gain_two * dn2
    d_resid = (
        dy_own
        + recip_own * weighted_two
        - resid_own * recip_own**3 * jnp.mean(weighted_two * resid_own, axis=1, keepdims=True)
    )
    d_resid_low = d_resid.astype(BF)
    d_mixed_all = cols_inner(d_resid_low, out_full).astype(BF)
    d_mixed = lax.all_to_all(d_mixed_all, "head", split_axis=1, concat_axis=0, tiled=True).astype(
        F32
    )
    d_out_part = rows_inner(mixed_own, d_resid_low).astype(BF)
    d_out_head = lax.psum_scatter(d_out_part, "head", scatter_dimension=0, tiled=True)
    d_attended = (d_mixed * gate_vals).astype(BF)
    d_gate_logit = (d_mixed * attended * gate_vals * (1.0 - gate_vals)).astype(BF)
    delta = jnp.zeros((row_count,), F32)
    for block_index in range(block_total):

        def delta_add(running, block_index=block_index):
            probs, key_block, value_block = probs_of(block_index)
            return running + jnp.sum(probs * cols_inner(d_attended, value_block), axis=1)

        delta = lax.cond(is_live(block_index), delta_add, keep_same, delta)
    d_queries = jnp.zeros((row_count, head_size), F32)
    grad_pieces = []
    for block_index in range(block_total):

        def block_grads(running, block_index=block_index):
            probs, key_block, value_block = probs_of(block_index)
            d_probs = cols_inner(d_attended, value_block)
            d_scores = (probs * (d_probs - delta[:, None]) * scale_factor).astype(BF)
            d_key_block = rows_inner(d_scores, queries)
            d_value_block = rows_inner(probs.astype(BF), d_attended)
            return (
                running + matmul(d_scores, key_block),
                jnp.concatenate([d_key_block, d_value_block], axis=1).astype(BF),
            )

        def block_empty(running):
            return (running, jnp.zeros((block_rows, 2 * head_size), BF))

        d_queries, grad_piece = lax.cond(is_live(block_index), block_grads, block_empty, d_queries)
        grad_pieces.append(grad_piece)
    d_kv_all = jnp.concatenate(grad_pieces, axis=0)
    d_kv_own = lax.psum_scatter(d_kv_all, "batch", scatter_dimension=0, tiled=True)
    d_kv_mate = from_partner(d_kv_own, "head")
    d_kv = (d_kv_own.astype(F32) + d_kv_mate.astype(F32)).astype(BF)
    d_cat = jnp.concatenate(
        [
            d_queries.astype(BF),
            jnp.where(first, d_kv[:, :half], d_kv[:, half:head_size]),
            jnp.where(first, d_kv[:, head_size : head_size + half], d_kv[:, head_size + half :]),
            d_gate_logit,
        ],
        axis=1,
    )
    w_key_own = jnp.where(
        first, w_in[:, head_size : head_size + half], w_in[:, head_size + half : 2 * head_size]
    )
    w_value_own = jnp.where(
        first,
        w_in[:, 2 * head_size : 2 * head_size + half],
        w_in[:, 2 * head_size + half : 3 * head_size],
    )
    w_cat = jnp.concatenate(
        [w_in[:, :head_size], w_key_own, w_value_own, w_in[:, 3 * head_size :]], axis=1
    )
    dn1_part = cols_inner(d_cat, w_cat).astype(BF)
    dn1 = lax.psum_scatter(dn1_part, "head", scatter_dimension=0, tiled=True).astype(F32)
    inputs_own = lax.dynamic_slice_in_dim(inputs, me * chunk, chunk, 0)
    recip_in = lax.dynamic_slice_in_dim(recip_one, me * chunk, chunk, 0)
    d_gain_one = jnp.sum(dn1 * inputs_own * recip_in, axis=0)
    weighted_one = gain_one * dn1
    d_tokens = (
        d_resid
        + recip_in * weighted_one
        - inputs_own * recip_in**3 * jnp.mean(weighted_one * inputs_own, axis=1, keepdims=True)
    ).astype(BF)
    d_tokens = lax.all_gather(d_tokens, "head", axis=0, tiled=True)
    d_mlp = jnp.concatenate(
        [
            rows_inner(normed_two, d_gate_pre).astype(BF),
            rows_inner(normed_two, d_up_pre).astype(BF),
        ],
        1,
    )
    d_mlp = lax.psum_scatter(d_mlp, "batch", scatter_dimension=0, tiled=True).astype(F32)
    d_down = rows_inner(hidden, out_grad).astype(BF)
    d_down = lax.psum_scatter(d_down, "batch", scatter_dimension=1, tiled=True).astype(F32)
    d_in = rows_inner(normed_one, d_cat).astype(BF)
    d_in = lax.psum_scatter(d_in, "batch", scatter_dimension=0, tiled=True).astype(F32)
    d_out = lax.psum_scatter(d_out_head, "batch", scatter_dimension=1, tiled=True).astype(F32)
    d_gains = lax.psum(jnp.stack([d_gain_one, d_gain_two]), ("batch", "head"))
    d_gains = lax.dynamic_slice_in_dim(
        d_gains, lax.axis_index("batch") * norm1_gain.shape[0], norm1_gain.shape[0], 1
    )
    hidden_own = w_mlp_gate.shape[1]
    return (
        output,
        d_tokens,
        d_gains[0],
        d_in[:, :head_size],
        d_in[:, head_size : head_size + half],
        d_in[:, head_size + half : 2 * head_size],
        d_in[:, 2 * head_size :],
        d_out,
        d_gains[1],
        d_mlp[:, :hidden_own],
        d_mlp[:, hidden_own:],
        d_down,
    )


def solution(mesh):
    return jax.shard_map(
        per_device,
        mesh=mesh,
        in_specs=(
            P("batch", None),
            P("batch"),
            P("batch"),
            P("batch", "head"),
            P("batch", "head"),
            P("batch", "head"),
            P("batch", "head"),
            P("head", "batch"),
            P("batch"),
            P("batch", "head"),
            P("batch", "head"),
            P("head", "batch"),
            P("batch", None),
        ),
        out_specs=(
            P("batch", None),
            P("batch", None),
            P("batch"),
            P("batch", "head"),
            P("batch", "head"),
            P("batch", "head"),
            P("batch", "head"),
            P("head", "batch"),
            P("batch"),
            P("batch", "head"),
            P("batch", "head"),
            P("head", "batch"),
        ),
        check_vma=False,
    )
```

profile of v0, /device:TPU:0, one launch (start us, length us, event | category | flops | bytes accessed | tf_op | source)
XLA Modules:
  0.0 1231.5 jit_solution(9865374111591020541)
XLA Ops:
  28.6 13.7 %all-gather.11.cloned.1.call-done = bf16[2048,512]{1,0:T(8,128)(2,1)} async-done(((bf16[512,512]{1,0:T(8,128)(2,1)}), bf16[2048,512]{1,0:T(8,128)(2,1)}) %all-gather.11.cloned.1.call-update) | async-done | bytes 2097168 | tf_op jit(solution)/shard_map/all_gather | solution.py:78
  99.6 52.8 %all-gather.17.cloned.1.call-done = bf16[1024,2048]{1,0:T(8,128)(2,1)} async-done(((bf16[128,2048]{1,0:T(8,128)(2,1)}), bf16[1024,2048]{1,0:T(8,128)(2,1)}) %all-gather.17.cloned.1.call-update) | async-done | bytes 4194320 | tf_op jit(solution)/shard_map/all_gather | solution.py:83
  152.4 55.6 %all-gather.15.cloned.1.call-done = bf16[1280,1024]{0,1:T(8,128)(2,1)} async-done(((bf16[1280,128]{0,1:T(8,128)(2,1)}), bf16[1280,1024]{0,1:T(8,128)(2,1)}) %all-gather.15.cloned.1.call-update) | async-done | bytes 2621456 | tf_op jit(solution)/shard_map/all_gather | solution.py:149
  208.0 10.4 multiply_reduce_fusion
  225.6 10.9 all-gather.19.cloned.1.call-done
  236.5 9.6 fusion.168
  246.2 20.4 %all-gather.21.cloned.1.call-done = bf16[2048,768]{1,0:T(8,128)(2,1)} async-done(((bf16[512,768]{1,0:T(8,128)(2,1)}), bf16[2048,768]{1,0:T(8,128)(2,1)}) %all-gather.21.cloned.1.call-update) | async-done | bytes 3145744 | tf_op jit(solution)/shard_map/all_gather | solution.py:85
  276.1 20.6 %all-gather.23.cloned.1.call-done = bf16[768,2048]{1,0:T(8,128)(2,1)} async-done(((bf16[768,512]{1,0:T(8,128)(2,1)}), bf16[768,2048]{1,0:T(8,128)(2,1)}) %all-gather.23.cloned.1.call-update) | async-done | bytes 3145744 | tf_op jit(solution)/shard_map/all_gather | solution.py:86
  296.6 13.6 %multiply_convert_fusion.2 = (bf16[1280,768]{1,0:T(8,128)(2,1)}, bf16[1280,768]{1,0:T(8,128)(2,1)}, bf16[1280,768]{1,0:T(8,128)(2,1)S(1)}) fusion(f32[1280,768]{1,0:T(8,128)} %fusion.168, f32[1280,768]{1,0:T(8,128)} %fusion.169, bf16[1280,2048]{1,0:T(8,128)(2,1)} %param.57, bf16[768,2048]{1,0:T(8,128)(2,1)} %all-gather.23.cloned.1.call-done), kind=kOutput, calls=%fused_computation.193 | convolution fusion | flops 4041277440 | bytes 22151168 | tf_op jit(solution)/shard_map/dot_general | solution.py:28
  332.7 94.8 %reduce-scatter.12.cloned.1.call-done = bf16[160,2048]{1,0:T(8,128)(2,1)} async-done(((bf16[1280,2048]{1,0:T(8,128)(2,1)}), bf16[160,2048]{1,0:T(8,128)(2,1)}) %reduce-scatter.12.cloned.1.call-update) | async-done | bytes 655376 | tf_op jit(solution)/shard_map/reduce_scatter | solution.py:166
  429.9 103.4 %reduce-scatter.10.cloned.1.call-done = bf16[160,2048]{1,0:T(8,128)(2,1)} async-done(((bf16[1280,2048]{1,0:T(8,128)(2,1)}), bf16[160,2048]{1,0:T(8,128)(2,1)}) %reduce-scatter.10.cloned.1.call-update) | async-done | bytes 655376 | tf_op jit(solution)/shard_map/reduce_scatter | solution.py:168
  544.6 10.4 all-to-all-done
  568.8 18.2 %conditional.28 = (f32[1280,128]{1,0:T(8,128)}, bf16[1280,256]{0,1:T(8,128)(2,1)}) conditional(s32[]{:T(128)} %bitcast.4, () %tuple.134, (s32[1280]{0:T(1024)S(1)}, s32[5120]{0:T(1024)S(1)}, s32[1280]{0:T(1024)S(1)}, bf16[5120,256]{0,1:T(8,128)(2,1)S(1)}, bf16[1280,128]{0,1:T(8,128)(2,1)S(1)}, /*index=5*/f32[1280]{0:T(1024)S(1)}, ...), branch_computations={%region_41.42_spmd, %region_42.43_spmd} | conditional | flops 2116812800 | bytes 39685136 | solution.py:212
  608.9 74.5 %reduce-scatter.14.cloned.1.call-done = bf16[1280,256]{0,1:T(8,128)(2,1)} async-done(((bf16[5120,256]{0,1:T(8,128)(2,1)}), bf16[1280,256]{0,1:T(8,128)(2,1)}) %reduce-scatter.14.cloned.1.call-update) | async-done | bytes 655376 | tf_op jit(solution)/shard_map/reduce_scatter | solution.py:215
  691.9 12.9 %collective-permute-done.1 = bf16[1280,256]{0,1:T(8,128)(2,1)S(1)} collective-permute-done((bf16[1280,256]{0,1:T(8,128)(2,1)}, bf16[1280,256]{0,1:T(8,128)(2,1)S(1)}, u32[]{:S(2)}, u32[]{:S(2)}) %collective-permute-start.1) | collective-permute-done | bytes 655392 | tf_op jit(solution)/shard_map/ppermute | solution.py:16
  740.8 35.7 %reduce-scatter.20.cloned.1.call-done = bf16[128,2048]{1,0:T(8,128)(2,1)} async-done(((bf16[1024,2048]{1,0:T(8,128)(2,1)}), bf16[128,2048]{1,0:T(8,128)(2,1)}) %reduce-scatter.20.cloned.1.call-update) | async-done | bytes 524304 | tf_op jit(solution)/shard_map/reduce_scatter | solution.py:183
  791.9 91.0 %reduce-scatter.16.cloned.1.call-done = bf16[160,2048]{1,0:T(8,128)(2,1)} async-done(((bf16[1280,2048]{1,0:T(8,128)(2,1)}), bf16[160,2048]{1,0:T(8,128)(2,1)}) %reduce-scatter.16.cloned.1.call-update) | async-done | bytes 655376 | tf_op jit(solution)/shard_map/reduce_scatter | solution.py:239
  887.6 35.6 %reduce-scatter.26.cloned.1.call-done = bf16[768,512]{1,0:T(8,128)(2,1)} async-done(((bf16[768,2048]{1,0:T(8,128)(2,1)}), bf16[768,512]{1,0:T(8,128)(2,1)}) %reduce-scatter.26.cloned.1.call-update) | async-done | bytes 786448 | tf_op jit(solution)/shard_map/reduce_scatter | solution.py:259
  925.6 58.5 %reduce-scatter.24.cloned.1.call-done = bf16[512,1536]{0,1:T(8,128)(2,1)} async-done(((bf16[2048,1536]{0,1:T(8,128)(2,1)}), bf16[512,1536]{0,1:T(8,128)(2,1)}) %reduce-scatter.24.cloned.1.call-update) | async-done | bytes 1572880 | tf_op jit(solution)/shard_map/reduce_scatter | solution.py:257
  989.1 83.3 %all-gather.25.cloned.1.call-done = bf16[1280,2048]{1,0:T(8,128)(2,1)} async-done(((bf16[160,2048]{1,0:T(8,128)(2,1)}), bf16[1280,2048]{1,0:T(8,128)(2,1)}) %all-gather.25.cloned.1.call-update) | async-done | bytes 5242896 | tf_op jit(solution)/shard_map/all_gather | solution.py:169
  1072.4 22.2 %reduce-scatter.22.cloned.1.call-done = bf16[128,512]{1,0:T(8,128)(2,1)} async-done(((bf16[128,2048]{1,0:T(8,128)(2,1)}), bf16[128,512]{1,0:T(8,128)(2,1)}) %reduce-scatter.22.cloned.1.call-update) | async-done | bytes 131088 | tf_op jit(solution)/shard_map/reduce_scatter | solution.py:262
  1096.2 29.7 %reduce-scatter.18.cloned.1.call-done = bf16[512,384]{1,0:T(8,128)(2,1)} async-done(((bf16[2048,384]{1,0:T(8,128)(2,1)}), bf16[512,384]{1,0:T(8,128)(2,1)}) %reduce-scatter.18.cloned.1.call-update) | async-done | bytes 393232 | tf_op jit(solution)/shard_map/reduce_scatter | solution.py:261
  1130.4 41.0 %psum.7 = f32[2,2048]{1,0:T(2,128)S(1)} all-reduce(f32[2,2048]{1,0:T(2,128)S(1)} %pad_maximum_fusion.11), channel_id=1, replica_groups=mesh['batch'=4,'head'=8] {'batch','head'}, use_global_device_ids=true, to_apply=%region_54.55 | all-reduce | flops 4096 | bytes 32768 | tf_op jit(solution)/shard_map/psum | solution.py:263
  1172.1 44.2 %all-gather.27.cloned.1.call-done = bf16[1280,2048]{1,0:T(8,128)(2,1)} async-done(((bf16[160,2048]{1,0:T(8,128)(2,1)}), bf16[1280,2048]{1,0:T(8,128)(2,1)}) %all-gather.27.cloned.1.call-update) | async-done | bytes 5242896 | tf_op jit(solution)/shard_map/all_gather | solution.py:249
  (196 shorter events, 285.9 us)
Async XLA Ops:
  7.2 35.1 %all-gather.11.cloned.1.call-start = ((), (), s32[]{:S(2)}) async-start(), calls=%async_computation.10 | async-start | bytes 2621440 | tf_op jit(solution)/shard_map/all_gather | solution.py:78
  9.3 6.5 collective-permute-start
  18.1 58.8 %all-gather.13.cloned.1.call-start = ((), (), s32[]{:S(2)}) async-start(), calls=%async_computation.11 | async-start | bytes 3276800 | tf_op jit(solution)/shard_map/all_gather | solution.py:95
  51.0 101.4 %all-gather.17.cloned.1.call-start = ((), (), s32[]{:S(2)}) async-start(), calls=%async_computation.13 | async-start | bytes 4718592 | tf_op jit(solution)/shard_map/all_gather | solution.py:83
  58.7 149.3 %all-gather.15.cloned.1.call-start = ((), (), s32[]{:S(2)}) async-start(), calls=%async_computation.12 | async-start | bytes 2949120 | tf_op jit(solution)/shard_map/all_gather | solution.py:149
  95.4 123.0 %copy-start.4 = (f32[1280,128]{0,1:T(8,128)}, f32[1280,128]{0,1:T(8,128)S(1)}, u32[]{:S(2)}) copy-start(f32[1280,128]{0,1:T(8,128)S(1)} %get-tuple-element.854) | copy-start | bytes 1966084
  97.7 138.9 %all-gather.19.cloned.1.call-start = ((), (), s32[]{:S(2)}) async-start(), calls=%async_computation.14 | async-start | bytes 3932160 | tf_op jit(solution)/shard_map/all_gather | solution.py:84
  98.3 168.2 %all-gather.21.cloned.1.call-start = ((), (), s32[]{:S(2)}) async-start(), calls=%async_computation.15 | async-start | bytes 3932160 | tf_op jit(solution)/shard_map/all_gather | solution.py:85
  98.8 197.8 %all-gather.23.cloned.1.call-start = ((), (), s32[]{:S(2)}) async-start(), calls=%async_computation.16 | async-start | bytes 3932160 | tf_op jit(solution)/shard_map/all_gather | solution.py:86
  99.6 327.8 %reduce-scatter.12.cloned.1.call-start = ((), (), s32[]{:S(2)}) async-start(), calls=%async_computation.19 | async-start | bytes 5898240 | tf_op jit(solution)/shard_map/reduce_scatter | solution.py:166
  324.7 208.7 %reduce-scatter.10.cloned.1.call-start = ((), (), s32[]{:S(2)}) async-start(), calls=%async_computation.17 | async-start | bytes 5898240 | tf_op jit(solution)/shard_map/reduce_scatter | solution.py:168
  540.1 15.0 %all-to-all-start = ((bf16[160,8,128]{2,0,1:T(8,128)(2,1)}), bf16[160,8,128]{2,0,1:T(8,128)(2,1)S(1)}, u32[]{:S(2)}, u32[]{:S(2)}) async-start(bf16[160,8,128]{2,0,1:T(8,128)(2,1)} %bitcast.84), calls=%async_computation.2 | async-start | bytes 655360 | tf_op jit(solution)/shard_map/all_to_all | solution.py:179
  544.6 138.8 %reduce-scatter.14.cloned.1.call-start = ((), (), s32[]{:S(2)}) async-start(), calls=%async_computation.20 | async-start | bytes 3276800 | tf_op jit(solution)/shard_map/reduce_scatter | solution.py:215
  604.4 172.1 %reduce-scatter.20.cloned.1.call-start = ((), (), s32[]{:S(2)}) async-start(), calls=%async_computation.24 | async-start | bytes 4718592 | tf_op jit(solution)/shard_map/reduce_scatter | solution.py:183
  608.9 96.1 %copy-start.8 = (bf16[1280,128]{0,1:T(8,128)(2,1)S(1)}, bf16[1280,128]{0,1:T(8,128)(2,1)}, u32[]{:S(2)}) copy-start(bf16[1280,128]{0,1:T(8,128)(2,1)} %get-tuple-element.873) | copy-start | bytes 983044
  608.9 273.9 %reduce-scatter.16.cloned.1.call-start = ((), (), s32[]{:S(2)}) async-start(), calls=%async_computation.21 | async-start | bytes 5898240 | tf_op jit(solution)/shard_map/reduce_scatter | solution.py:239
  683.4 21.4 %collective-permute-start.1 = (bf16[1280,256]{0,1:T(8,128)(2,1)}, bf16[1280,256]{0,1:T(8,128)(2,1)S(1)}, u32[]{:S(2)}, u32[]{:S(2)}) collective-permute-start(bf16[1280,256]{0,1:T(8,128)(2,1)} %reduce-scatter.14.cloned.1.call-done), channel_id=1, source_target_pairs={{0,1},{1,0},{2,3},{3,2},{4,5},{5,4},{6,7},{7,6},{8,9},{9,8},{10,11... | collective-permute-start | bytes 1966088 | tf_op jit(solution)/shard_map/ppermute | solution.py:16
  711.9 211.2 %reduce-scatter.26.cloned.1.call-start = ((), (), s32[]{:S(2)}) async-start(), calls=%async_computation.27 | async-start | bytes 3932160 | tf_op jit(solution)/shard_map/reduce_scatter | solution.py:259
  721.5 262.5 %reduce-scatter.24.cloned.1.call-start = ((), (), s32[]{:S(2)}) async-start(), calls=%async_computation.26 | async-start | bytes 7864320 | tf_op jit(solution)/shard_map/reduce_scatter | solution.py:257
  740.2 332.2 %all-gather.25.cloned.1.call-start = ((), (), s32[]{:S(2)}) async-start(), calls=%async_computation.18 | async-start | bytes 5898240 | tf_op jit(solution)/shard_map/all_gather | solution.py:169
  740.8 353.8 %reduce-scatter.22.cloned.1.call-start = ((), (), s32[]{:S(2)}) async-start(), calls=%async_computation.25 | async-start | bytes 655360 | tf_op jit(solution)/shard_map/reduce_scatter | solution.py:262
  776.5 349.4 %reduce-scatter.18.cloned.1.call-start = ((), (), s32[]{:S(2)}) async-start(), calls=%async_computation.23 | async-start | bytes 1966080 | tf_op jit(solution)/shard_map/reduce_scatter | solution.py:261
  783.8 432.5 %all-gather.27.cloned.1.call-start = ((), (), s32[]{:S(2)}) async-start(), calls=%async_computation.22 | async-start | bytes 5898240 | tf_op jit(solution)/shard_map/all_gather | solution.py:249
  987.5 142.9 %copy-start.14 = (f32[2048]{0:T(1024)S(1)}, f32[2048]{0:T(1024)}, u32[]{:S(2)}) copy-start(f32[2048]{0:T(1024)} %get-tuple-element.857) | copy-start | bytes 24580
  (18 other events, 281.4 us)
Sparse Core Ops, SparseCore 0:
  18.2 24.0 all-gather.10
  51.1 25.6 all-gather.12
  79.0 73.4 all-gather.16
  155.0 52.9 all-gather.14
  209.4 27.0 all-gather.18
  237.9 28.5 all-gather.20
  268.1 28.5 all-gather.22
  324.8 102.5 reduce-scatter.11
  431.0 102.3 reduce-scatter.9
  604.5 78.8 reduce-scatter.13
  687.5 89.0 reduce-scatter.19
  780.5 102.2 reduce-scatter.15
  885.3 37.7 reduce-scatter.25
  925.7 58.3 reduce-scatter.23
  986.1 86.2 all-gather.24
  1074.8 19.7 reduce-scatter.21
  1097.7 28.1 reduce-scatter.17
  1128.6 87.6 all-gather.26
where the time goes:
time: 1240 us; the launch traced here: 1230 us
  waiting for transfers between devices  879 us (71%)
  matrix products  137 us (11%)
  blocking collectives  59.1 us (5%)
  other arithmetic  52.6 us (4%)
  local copies, waits for them, and re-layouts  51.9 us (4%)
  between operations  22.7 us (2%)
  loops' own time  18.7 us (2%)
    reduce_scatter x1, waiting for transfers between devices, per_device(): lax.psum_scatter(mlp_part, 'head', scatter_dimension=0, tiled=True)  103 us
    reduce_scatter x1, waiting for transfers between devices, per_device(): lax.psum_scatter(dn2_part.astype(BF), 'head', scatter_dimension=0, tiled=...  94.8 us
    reduce_scatter x1, waiting for transfers between devices, per_device(): lax.psum_scatter(dn1_part, 'head', scatter_dimension=0, tiled=True)  91 us
    all_gather x1, waiting for transfers between devices, per_device(): lax.all_gather((resid_own + mlp_own).astype(BF), 'head', axis=0, tiled=True)  83.3 us
    reduce_scatter x1, waiting for transfers between devices, per_device(): lax.psum_scatter(d_kv_all, 'batch', scatter_dimension=0, tiled=True)  74.5 us
    reduce_scatter x1, waiting for transfers between devices, per_device(): lax.psum_scatter(d_mlp, 'batch', scatter_dimension=0, tiled=True)  58.5 us
    all_gather x1, waiting for transfers between devices, per_device(): mixed_all = lax.all_gather(mixed, 'head', axis=1, tiled=True)  55.6 us
    all_gather x1, waiting for transfers between devices, per_device(): out_full = lax.all_gather(out_own, 'head', axis=0, tiled=True)  52.8 us
  transfers between devices with their start and end apart: 21, of which 21 were waited for; matrix products, arithmetic and copies ran while one was open for 12% of the time, Pallas kernels for 0%

commit v1 on v0

--- a/solution.py
+++ b/solution.py
@@ -8,6 +8,27 @@
 MASKED = -1e30
 BF = jnp.bfloat16
 F32 = jnp.float32
+
+
+def collect(x, axis, dim):
+    length, index, rows = (lax.axis_size(axis), lax.axis_index(axis), x.shape[dim])
+    forward = [(i, (i + 1) % length) for i in range(length)]
+    left = [(i, (i - 1) % length) for i in range(length)]
+    out = jnp.zeros((*x.shape[:dim], length * rows, *x.shape[dim + 1 :]), x.dtype)
+    out = lax.dynamic_update_slice_in_dim(out, x, index * rows, axis=dim)
+    from_left = from_right = x
+    half = length // 2
+    for lap in range(1, half + 1):
+        from_left = lax.ppermute(from_left, axis, forward)
+        out = lax.dynamic_update_slice_in_dim(
+            out, from_left, (index - lap) % length * rows, axis=dim
+        )
+        if lap < length - half:
+            from_right = lax.ppermute(from_right, axis, left)
+            out = lax.dynamic_update_slice_in_dim(
+                out, from_right, (index + lap) % length * rows, axis=dim
+            )
+    return out
 
 
 def from_partner(block, axis):
@@ -166,7 +187,7 @@
     dn2 = lax.psum_scatter(dn2_part.astype(BF), "head", scatter_dimension=0, tiled=True).astype(F32)
     mlp_part = matmul(hidden, down_full).astype(BF)
     mlp_own = lax.psum_scatter(mlp_part, "head", scatter_dimension=0, tiled=True).astype(F32)
-    output = lax.all_gather((resid_own + mlp_own).astype(BF), "head", axis=0, tiled=True)
+    output = collect((resid_own + mlp_own).astype(BF), "head", 0)
     d_gain_two = jnp.sum(dn2 * resid_own * recip_own, axis=0)
     weighted_two = gain_two * dn2
     d_resid = (

time: 1240 us -> 1150 us (0.927)
  waiting for transfers between devices: 879 us -> 772 us
  starting transfers between devices: 10.3 us -> 27.3 us
    all_gather x1 -> x0, waiting for transfers between devices: 83.3 us -> none  [per_device(): lax.all_gather((resid_own + mlp_own).astype(BF), 'head', axis=0, tiled=True)]
    ppermute x0 -> x7, waiting for transfers between devices: none -> 71.5 us  [the longest x4 71.5 us: collect(): from_left = lax.ppermute(from_left, axis, forward)]
    reduce_scatter x1, waiting for transfers between devices: 58.5 us -> 2.55 us  [per_device(): lax.psum_scatter(d_mlp, 'batch', scatter_dimension=0, tiled=True)]
    reduce_scatter x1, waiting for transfers between devices: 35.6 us -> 0.78 us  [per_device(): lax.psum_scatter(d_down, 'batch', scatter_dimension=1, tiled=True)]
    ppermute x0 -> x7, starting transfers between devices: none -> 16.8 us  [the longest x4 9.04 us: collect(): from_left = lax.ppermute(from_left, axis, forward)]
  transfers between devices with their start and end apart: 21 -> 27, of which waited for: 21 -> 24; matrix products, arithmetic and copies ran while one was open for 12% -> 14% of each run, Pallas kernels for 0% -> 0%
where the time goes in v1:
time: 1150 us; the launch traced here: 1140 us
  waiting for transfers between devices  772 us (67%)
  matrix products  136 us (12%)
  local copies, waits for them, and re-layouts  60.9 us (5%)
  blocking collectives  59 us (5%)
  other arithmetic  53.6 us (5%)
  starting transfers between devices  27.3 us (2%)
  between operations  22.4 us (2%)
    reduce_scatter x1, waiting for transfers between devices, per_device(): lax.psum_scatter(dn2_part.astype(BF), 'head', scatter_dimension=0, tiled=...  103 us
    reduce_scatter x1, waiting for transfers between devices, per_device(): lax.psum_scatter(mlp_part, 'head', scatter_dimension=0, tiled=True)  102 us
    reduce_scatter x1, waiting for transfers between devices, per_device(): lax.psum_scatter(dn1_part, 'head', scatter_dimension=0, tiled=True)  90.7 us
    reduce_scatter x1, waiting for transfers between devices, per_device(): lax.psum_scatter(d_kv_all, 'batch', scatter_dimension=0, tiled=True)  83.5 us
    ppermute x4, waiting for transfers between devices, collect(): from_left = lax.ppermute(from_left, axis, forward)  71.5 us
    all_gather x1, waiting for transfers between devices, per_device(): mixed_all = lax.all_gather(mixed, 'head', axis=1, tiled=True)  55.6 us
    all_gather x1, waiting for transfers between devices, per_device(): out_full = lax.all_gather(out_own, 'head', axis=0, tiled=True)  52.8 us
    dot_general x7, matrix products, matmul(): return jnp.dot(left, right, preferred_element_type=F32)  52.7 us
  transfers between devices with their start and end apart: 27, of which 24 were waited for; matrix products, arithmetic and copies ran while one was open for 14% of the time, Pallas kernels for 0%

profile of v1, /device:TPU:0, one launch (start us, length us, event | category | flops | bytes accessed | tf_op | source)
XLA Modules:
  0.0 1140.4 jit_solution(11310236427097215450)
XLA Ops:
  28.6 13.7 %all-gather.10.cloned.1.call-done = bf16[2048,512]{1,0:T(8,128)(2,1)} async-done(((bf16[512,512]{1,0:T(8,128)(2,1)}), bf16[2048,512]{1,0:T(8,128)(2,1)}) %all-gather.10.cloned.1.call-update) | async-done | bytes 2097168 | tf_op jit(solution)/shard_map/all_gather | solution.py:99
  99.7 52.8 %all-gather.16.cloned.1.call-done = bf16[1024,2048]{1,0:T(8,128)(2,1)} async-done(((bf16[128,2048]{1,0:T(8,128)(2,1)}), bf16[1024,2048]{1,0:T(8,128)(2,1)}) %all-gather.16.cloned.1.call-update) | async-done | bytes 4194320 | tf_op jit(solution)/shard_map/all_gather | solution.py:104
  152.5 55.6 %all-gather.14.cloned.1.call-done = bf16[1280,1024]{0,1:T(8,128)(2,1)} async-done(((bf16[1280,128]{0,1:T(8,128)(2,1)}), bf16[1280,1024]{0,1:T(8,128)(2,1)}) %all-gather.14.cloned.1.call-update) | async-done | bytes 2621456 | tf_op jit(solution)/shard_map/all_gather | solution.py:170
  208.0 10.4 multiply_reduce_fusion
  225.7 10.8 all-gather.18.cloned.1.call-done
  236.6 9.6 fusion.168
  246.2 20.4 %all-gather.20.cloned.1.call-done = bf16[2048,768]{1,0:T(8,128)(2,1)} async-done(((bf16[512,768]{1,0:T(8,128)(2,1)}), bf16[2048,768]{1,0:T(8,128)(2,1)}) %all-gather.20.cloned.1.call-update) | async-done | bytes 3145744 | tf_op jit(solution)/shard_map/all_gather | solution.py:106
  276.1 20.5 %all-gather.22.cloned.1.call-done = bf16[768,2048]{1,0:T(8,128)(2,1)} async-done(((bf16[768,512]{1,0:T(8,128)(2,1)}), bf16[768,2048]{1,0:T(8,128)(2,1)}) %all-gather.22.cloned.1.call-update) | async-done | bytes 3145744 | tf_op jit(solution)/shard_map/all_gather | solution.py:107
  296.7 13.6 %multiply_convert_fusion.2 = (bf16[1280,768]{1,0:T(8,128)(2,1)}, bf16[1280,768]{1,0:T(8,128)(2,1)S(1)}, bf16[1280,768]{1,0:T(8,128)(2,1)}) fusion(f32[1280,768]{1,0:T(8,128)} %fusion.168, f32[1280,768]{1,0:T(8,128)} %fusion.169, bf16[1280,2048]{1,0:T(8,128)(2,1)} %param.57, bf16[768,2048]{1,0:T(8,128)(2,1)} %all-gather.22.cloned.1.call-done), kind=kOutput, calls=%fused_computation.193 | convolution fusion | flops 4041277440 | bytes 22151168 | tf_op jit(solution)/shard_map/dot_general | solution.py:49
  322.5 102.7 %reduce-scatter.12.cloned.1.call-done = bf16[160,2048]{1,0:T(8,128)(2,1)} async-done(((bf16[1280,2048]{1,0:T(8,128)(2,1)}), bf16[160,2048]{1,0:T(8,128)(2,1)}) %reduce-scatter.12.cloned.1.call-update) | async-done | bytes 655376 | tf_op jit(solution)/shard_map/reduce_scatter | solution.py:187
  437.8 10.4 all-to-all-done
  462.2 13.4 %conditional.28 = (f32[1280,128]{1,0:T(8,128)}, bf16[1280,256]{0,1:T(8,128)(2,1)}) conditional(s32[]{:T(128)} %bitcast.4, () %tuple.134, (s32[1280]{0:T(1024)S(1)}, s32[5120]{0:T(1024)S(1)}, s32[1280]{0:T(1024)S(1)}, bf16[5120,256]{0,1:T(8,128)(2,1)S(1)}, bf16[1280,128]{0,1:T(8,128)(2,1)S(1)}, /*index=5*/f32[1280]{0:T(1024)S(1)}, ...), branch_computations={%region_41.42_spmd, %region_42.43_spmd} | conditional | flops 2116812800 | bytes 39685136 | solution.py:233
  492.5 83.5 %reduce-scatter.14.cloned.1.call-done = bf16[1280,256]{0,1:T(8,128)(2,1)} async-done(((bf16[5120,256]{0,1:T(8,128)(2,1)}), bf16[1280,256]{0,1:T(8,128)(2,1)}) %reduce-scatter.14.cloned.1.call-update) | async-done | bytes 655376 | tf_op jit(solution)/shard_map/reduce_scatter | solution.py:236
  584.5 13.0 %collective-permute-done.8 = bf16[1280,256]{0,1:T(8,128)(2,1)S(1)} collective-permute-done((bf16[1280,256]{0,1:T(8,128)(2,1)}, bf16[1280,256]{0,1:T(8,128)(2,1)S(1)}, u32[]{:S(2)}, u32[]{:S(2)}) %collective-permute-start.8) | collective-permute-done | bytes 655392 | tf_op jit(solution)/shard_map/ppermute | solution.py:37
  642.3 26.8 %reduce-scatter.20.cloned.1.call-done = bf16[128,2048]{1,0:T(8,128)(2,1)} async-done(((bf16[1024,2048]{1,0:T(8,128)(2,1)}), bf16[128,2048]{1,0:T(8,128)(2,1)}) %reduce-scatter.20.cloned.1.call-update) | async-done | bytes 524304 | tf_op jit(solution)/shard_map/reduce_scatter | solution.py:204
  684.4 90.7 %reduce-scatter.16.cloned.1.call-done = bf16[160,2048]{1,0:T(8,128)(2,1)} async-done(((bf16[1280,2048]{1,0:T(8,128)(2,1)}), bf16[160,2048]{1,0:T(8,128)(2,1)}) %reduce-scatter.16.cloned.1.call-update) | async-done | bytes 655376 | tf_op jit(solution)/shard_map/reduce_scatter | solution.py:260
  779.8 101.6 %reduce-scatter.10.cloned.1.call-done = bf16[160,2048]{1,0:T(8,128)(2,1)} async-done(((bf16[1280,2048]{1,0:T(8,128)(2,1)}), bf16[160,2048]{1,0:T(8,128)(2,1)}) %reduce-scatter.10.cloned.1.call-update) | async-done | bytes 655376 | tf_op jit(solution)/shard_map/reduce_scatter | solution.py:189
  891.5 24.7 %collective-permute-done.1 = bf16[160,2048]{1,0:T(8,128)(2,1)S(1)} collective-permute-done((bf16[160,2048]{1,0:T(8,128)(2,1)S(1)}, bf16[160,2048]{1,0:T(8,128)(2,1)S(1)}, u32[]{:S(2)}, u32[]{:S(2)}) %collective-permute-start.1) | collective-permute-done | bytes 655392 | tf_op jit(solution)/shard_map/ppermute | solution.py:22
  925.0 20.7 %collective-permute-done.3 = bf16[160,2048]{1,0:T(8,128)(2,1)S(1)} collective-permute-done((bf16[160,2048]{1,0:T(8,128)(2,1)S(1)}, bf16[160,2048]{1,0:T(8,128)(2,1)S(1)}, u32[]{:S(2)}, u32[]{:S(2)}) %collective-permute-start.3) | collective-permute-done | bytes 655392 | tf_op jit(solution)/shard_map/ppermute | solution.py:22
  953.2 21.4 %collective-permute-done.5 = bf16[160,2048]{1,0:T(8,128)(2,1)} collective-permute-done((bf16[160,2048]{1,0:T(8,128)(2,1)S(1)}, bf16[160,2048]{1,0:T(8,128)(2,1)}, u32[]{:S(2)}, u32[]{:S(2)}) %collective-permute-start.5) | collective-permute-done | bytes 655392 | tf_op jit(solution)/shard_map/ppermute | solution.py:22
  994.4 12.3 %reduce-scatter.22.cloned.1.call-done = bf16[128,512]{1,0:T(8,128)(2,1)} async-done(((bf16[128,2048]{1,0:T(8,128)(2,1)}), bf16[128,512]{1,0:T(8,128)(2,1)}) %reduce-scatter.22.cloned.1.call-update) | async-done | bytes 131088 | tf_op jit(solution)/shard_map/reduce_scatter | solution.py:283
  1008.3 29.7 %reduce-scatter.18.cloned.1.call-done = bf16[512,384]{1,0:T(8,128)(2,1)} async-done(((bf16[2048,384]{1,0:T(8,128)(2,1)}), bf16[512,384]{1,0:T(8,128)(2,1)}) %reduce-scatter.18.cloned.1.call-update) | async-done | bytes 393232 | tf_op jit(solution)/shard_map/reduce_scatter | solution.py:282
  1042.4 40.9 %psum.7 = f32[2,2048]{1,0:T(2,128)S(1)} all-reduce(f32[2,2048]{1,0:T(2,128)S(1)} %pad_maximum_fusion.11), channel_id=1, replica_groups=mesh['batch'=4,'head'=8] {'batch','head'}, use_global_device_ids=true, to_apply=%region_54.55 | all-reduce | flops 4096 | bytes 32768 | tf_op jit(solution)/shard_map/psum | solution.py:284
  1084.0 43.9 %all-gather.24.cloned.1.call-done = bf16[1280,2048]{1,0:T(8,128)(2,1)} async-done(((bf16[160,2048]{1,0:T(8,128)(2,1)}), bf16[1280,2048]{1,0:T(8,128)(2,1)}) %all-gather.24.cloned.1.call-update) | async-done | bytes 5242896 | tf_op jit(solution)/shard_map/all_gather | solution.py:270
  (215 shorter events, 314.7 us)
Async XLA Ops:
  7.2 35.1 %all-gather.10.cloned.1.call-start = ((), (), s32[]{:S(2)}) async-start(), calls=%async_computation.10 | async-start | bytes 2621440 | tf_op jit(solution)/shard_map/all_gather | solution.py:99
  18.1 58.8 %all-gather.12.cloned.1.call-start = ((), (), s32[]{:S(2)}) async-start(), calls=%async_computation.11 | async-start | bytes 3276800 | tf_op jit(solution)/shard_map/all_gather | solution.py:116
  51.0 101.4 %all-gather.16.cloned.1.call-start = ((), (), s32[]{:S(2)}) async-start(), calls=%async_computation.13 | async-start | bytes 4718592 | tf_op jit(solution)/shard_map/all_gather | solution.py:104
  58.8 149.3 %all-gather.14.cloned.1.call-start = ((), (), s32[]{:S(2)}) async-start(), calls=%async_computation.12 | async-start | bytes 2949120 | tf_op jit(solution)/shard_map/all_gather | solution.py:170
  97.7 138.8 %all-gather.18.cloned.1.call-start = ((), (), s32[]{:S(2)}) async-start(), calls=%async_computation.14 | async-start | bytes 3932160 | tf_op jit(solution)/shard_map/all_gather | solution.py:105
  98.3 168.2 %all-gather.20.cloned.1.call-start = ((), (), s32[]{:S(2)}) async-start(), calls=%async_computation.15 | async-start | bytes 3932160 | tf_op jit(solution)/shard_map/all_gather | solution.py:106
  98.9 197.8 %all-gather.22.cloned.1.call-start = ((), (), s32[]{:S(2)}) async-start(), calls=%async_computation.16 | async-start | bytes 3932160 | tf_op jit(solution)/shard_map/all_gather | solution.py:107
  99.6 325.5 %reduce-scatter.12.cloned.1.call-start = ((), (), s32[]{:S(2)}) async-start(), calls=%async_computation.18 | async-start | bytes 5898240 | tf_op jit(solution)/shard_map/reduce_scatter | solution.py:187
  437.8 138.3 %reduce-scatter.14.cloned.1.call-start = ((), (), s32[]{:S(2)}) async-start(), calls=%async_computation.19 | async-start | bytes 3276800 | tf_op jit(solution)/shard_map/reduce_scatter | solution.py:236
  487.9 181.3 %reduce-scatter.20.cloned.1.call-start = ((), (), s32[]{:S(2)}) async-start(), calls=%async_computation.23 | async-start | bytes 4718592 | tf_op jit(solution)/shard_map/reduce_scatter | solution.py:204
  492.5 282.6 %reduce-scatter.16.cloned.1.call-start = ((), (), s32[]{:S(2)}) async-start(), calls=%async_computation.20 | async-start | bytes 5898240 | tf_op jit(solution)/shard_map/reduce_scatter | solution.py:260
  576.1 21.4 %collective-permute-start.8 = (bf16[1280,256]{0,1:T(8,128)(2,1)}, bf16[1280,256]{0,1:T(8,128)(2,1)S(1)}, u32[]{:S(2)}, u32[]{:S(2)}) collective-permute-start(bf16[1280,256]{0,1:T(8,128)(2,1)} %reduce-scatter.14.cloned.1.call-done), channel_id=1, source_target_pairs={{0,1},{1,0},{2,3},{3,2},{4,5},{5,4},{6,7},{7,6},{8,9},{9,8},{10,11... | collective-permute-start | bytes 1966088 | tf_op jit(solution)/shard_map/ppermute | solution.py:37
  604.5 276.9 %reduce-scatter.10.cloned.1.call-start = ((), (), s32[]{:S(2)}) async-start(), calls=%async_computation.17 | async-start | bytes 5898240 | tf_op jit(solution)/shard_map/reduce_scatter | solution.py:189
  614.2 307.5 %reduce-scatter.26.cloned.1.call-start = ((), (), s32[]{:S(2)}) async-start(), calls=%async_computation.26 | async-start | bytes 3932160 | tf_op jit(solution)/shard_map/reduce_scatter | solution.py:280
  623.3 359.3 %reduce-scatter.24.cloned.1.call-start = ((), (), s32[]{:S(2)}) async-start(), calls=%async_computation.25 | async-start | bytes 7864320 | tf_op jit(solution)/shard_map/reduce_scatter | solution.py:278
  642.3 364.4 %reduce-scatter.22.cloned.1.call-start = ((), (), s32[]{:S(2)}) async-start(), calls=%async_computation.24 | async-start | bytes 655360 | tf_op jit(solution)/shard_map/reduce_scatter | solution.py:283
  669.2 368.8 %reduce-scatter.18.cloned.1.call-start = ((), (), s32[]{:S(2)}) async-start(), calls=%async_computation.22 | async-start | bytes 1966080 | tf_op jit(solution)/shard_map/reduce_scatter | solution.py:282
  676.2 451.7 %all-gather.24.cloned.1.call-start = ((), (), s32[]{:S(2)}) async-start(), calls=%async_computation.21 | async-start | bytes 5898240 | tf_op jit(solution)/shard_map/all_gather | solution.py:270
  886.7 29.4 %collective-permute-start.1 = (bf16[160,2048]{1,0:T(8,128)(2,1)S(1)}, bf16[160,2048]{1,0:T(8,128)(2,1)S(1)}, u32[]{:S(2)}, u32[]{:S(2)}) collective-permute-start(bf16[160,2048]{1,0:T(8,128)(2,1)S(1)} %get-tuple-element.860), channel_id=1, source_target_pairs={{0,1},{1,2},{2,3},{3,4},{4,5},{5,6},{6,7},{7,0},{8,9},{9,10},{10,1... | collective-permute-start | bytes 1966088 | tf_op jit(solution)/shard_map/ppermute | solution.py:22
  888.2 30.4 %collective-permute-start.2 = (bf16[160,2048]{1,0:T(8,128)(2,1)S(1)}, bf16[160,2048]{1,0:T(8,128)(2,1)S(1)}, u32[]{:S(2)}, u32[]{:S(2)}) collective-permute-start(bf16[160,2048]{1,0:T(8,128)(2,1)S(1)} %get-tuple-element.860), channel_id=1, source_target_pairs={{0,7},{1,0},{2,1},{3,2},{4,3},{5,4},{6,5},{7,6},{8,15},{9,8},{10,9... | collective-permute-start | bytes 1966088 | tf_op jit(solution)/shard_map/ppermute | solution.py:27
  916.1 29.6 %collective-permute-start.3 = (bf16[160,2048]{1,0:T(8,128)(2,1)S(1)}, bf16[160,2048]{1,0:T(8,128)(2,1)S(1)}, u32[]{:S(2)}, u32[]{:S(2)}) collective-permute-start(bf16[160,2048]{1,0:T(8,128)(2,1)S(1)} %collective-permute-done.1), channel_id=1, source_target_pairs={{0,1},{1,2},{2,3},{3,4},{4,5},{5,6},{6,7},{7,0},{8,9},{9,10},{10,1... | collective-permute-start | bytes 1966088 | tf_op jit(solution)/shard_map/ppermute | solution.py:22
  918.6 30.5 %collective-permute-start.4 = (bf16[160,2048]{1,0:T(8,128)(2,1)S(1)}, bf16[160,2048]{1,0:T(8,128)(2,1)S(1)}, u32[]{:S(2)}, u32[]{:S(2)}) collective-permute-start(bf16[160,2048]{1,0:T(8,128)(2,1)S(1)} %collective-permute-done.2), channel_id=1, source_target_pairs={{0,7},{1,0},{2,1},{3,2},{4,3},{5,4},{6,5},{7,6},{8,15},{9,8},{10,9... | collective-permute-start | bytes 1966088 | tf_op jit(solution)/shard_map/ppermute | solution.py:27
  945.8 28.8 %collective-permute-start.5 = (bf16[160,2048]{1,0:T(8,128)(2,1)S(1)}, bf16[160,2048]{1,0:T(8,128)(2,1)}, u32[]{:S(2)}, u32[]{:S(2)}) collective-permute-start(bf16[160,2048]{1,0:T(8,128)(2,1)S(1)} %collective-permute-done.3), channel_id=1, source_target_pairs={{0,1},{1,2},{2,3},{3,4},{4,5},{5,6},{6,7},{7,0},{8,9},{9,10},{10,1... | collective-permute-start | bytes 1966088 | tf_op jit(solution)/shard_map/ppermute | solution.py:22
  949.1 30.0 %collective-permute-start.6 = (bf16[160,2048]{1,0:T(8,128)(2,1)S(1)}, bf16[160,2048]{1,0:T(8,128)(2,1)S(1)}, u32[]{:S(2)}, u32[]{:S(2)}) collective-permute-start(bf16[160,2048]{1,0:T(8,128)(2,1)S(1)} %collective-permute-done.4), channel_id=1, source_target_pairs={{0,7},{1,0},{2,1},{3,2},{4,3},{5,4},{6,5},{7,6},{8,15},{9,8},{10,9... | collective-permute-start | bytes 1966088 | tf_op jit(solution)/shard_map/ppermute | solution.py:27
  (24 other events, 562.8 us)
Sparse Core Ops, SparseCore 0:
  18.2 24.0 all-gather.9
  51.1 25.6 all-gather.11
  79.0 73.4 all-gather.15
  155.1 52.9 all-gather.13
  209.4 27.0 all-gather.17
  238.0 28.5 all-gather.19
  268.1 28.5 all-gather.21
  322.5 102.5 reduce-scatter.11
  488.0 88.0 reduce-scatter.13
  580.0 89.1 reduce-scatter.19
  672.7 102.2 reduce-scatter.15
  779.1 102.2 reduce-scatter.9
  883.9 37.6 reduce-scatter.25
  924.2 58.3 reduce-scatter.23
  984.9 21.6 reduce-scatter.21
  1009.8 28.1 reduce-scatter.17
  1040.0 87.8 all-gather.23
